TPU v7x, 256 devices: a whole 4x4x8 slice. The times are simulated.
256 devices in a mesh: wide: 32 (over y_hi, z, core), narrow: 8 (over x, y_lo).
Axes of the slice: x: 4, y: 4 (y_hi: 2, y_lo: 2; y = y_hi * 2 + y_lo), z: 8, core: 2. Of those that a mesh axis runs over, the one named last changes fastest.
Arguments:
- matrix: float32 [16384, 16384], P('narrow', 'wide'), may hold values from -64 to 64
Outputs:
- rotated: float32 [16384, 16384], P('narrow', 'wide')
All inputs are finite; a program needn't handle non-finite values.
Results may differ from a plain program's by a relative error of at most 0.0003.
Values sent between devices are 32-bit elements; how exact they have to be, the bound alone decides.
No kernel may reach another device: no remote copies, remote signals or barrier semaphores. Data moves between devices by JAX's collectives and lax.ppermute only.
A program may use at most 64 MiB of HBM per device.

v0:
```python
import jax
import jax.numpy as jnp
from jax import lax
from jax.sharding import PartitionSpec as P

STEPS = 2


def from_behind(value, axis, steps):
    count = lax.axis_size(axis)
    pairs = [(source, (source + steps) % count) for source in range(count)]
    return lax.ppermute(value, axis, pairs)


def product(left, right):
    return jnp.dot(left, right, precision=lax.Precision.HIGHEST)


def spd_solve(factor_low, right_side):
    first_pass = lax.linalg.triangular_solve(factor_low, right_side, left_side=True, lower=True)
    return lax.linalg.triangular_solve(
        factor_low, first_pass, left_side=True, lower=True, transpose_a=True
    )


def turn_pair(upper_block, lower_block, cross_gram, upper_norms, lower_norms):
    damped = cross_gram / (upper_norms[:, None] + lower_norms[None, :])
    block_width = damped.shape[0]
    identity = jnp.eye(block_width, dtype=damped.dtype)
    left_square = product(damped, damped.T)
    left_factor = jnp.linalg.cholesky(identity + left_square)
    solved = spd_solve(left_factor, jnp.concatenate([identity, damped], axis=1))
    inverse = solved[:, :block_width]
    inverse_damped = solved[:, block_width:]
    keep_upper = 2.0 * inverse - identity
    into_lower = 2.0 * inverse_damped
    into_upper = -2.0 * inverse_damped.T
    keep_lower = identity - 2.0 * product(damped.T, inverse_damped)
    new_upper = product(upper_block, keep_upper) + product(lower_block, into_upper)
    new_lower = product(upper_block, into_lower) + product(lower_block, keep_lower)
    return (new_upper, new_lower)


def gram_terms(upper_block, pieces):
    block_width = upper_block.shape[1]
    whole_pair = jnp.concatenate((upper_block,) + pieces, axis=1)
    summed = lax.psum(product(whole_pair.T, whole_pair), "narrow")
    diagonal = jnp.diagonal(summed)
    return (summed[:block_width, block_width:], diagonal[:block_width], diagonal[block_width:])


def move_lower(lower_block):
    return (from_behind(lower_block, "wide", 1),)


def shards(matrix):
    block_width = matrix.shape[1] // 2
    upper_block = matrix[:, :block_width]
    pieces = (matrix[:, block_width:],)
    for step_index in range(STEPS):
        cross_gram, upper_norms, lower_norms = gram_terms(upper_block, pieces)
        lower_block = pieces[0]
        upper_block, lower_block = turn_pair(
            upper_block, lower_block, cross_gram, upper_norms, lower_norms
        )
        pieces = move_lower(lower_block)
    return jnp.concatenate((upper_block,) + pieces, axis=1)


def solution(mesh):
    in_specs = (P("narrow", "wide"),)
    out_specs = P("narrow", "wide")
    return jax.shard_map(shards, mesh=mesh, in_specs=in_specs, out_specs=out_specs, check_vma=False)
```

profile of v0, /device:TPU:16, one launch (start us, length us, event | category | flops | bytes accessed | tf_op | source)
XLA Modules:
  0.0 424.8 jit_solution(5533521235223102054)
XLA Ops:
  6.5 11.2 %fusion.69 = f32[512,512]{0,1:T(8,128)} fusion(f32[2048,512]{1,0:T(8,128)} %param.6), kind=kOutput, calls=%fused_computation.131 | convolution fusion | flops 6442450944 | bytes 5242880 | tf_op jit(solution)/shard_map/dot_general | solution.py:16
  18.1 85.3 %all-reduce.4.cloned.1.call-done = f32[512,512]{0,1:T(8,128)} async-done(((f32[512,512]{0,1:T(8,128)}), f32[512,512]{0,1:T(8,128)}) %all-reduce.4.cloned.1.call-update) | async-done | bytes 1048592 | tf_op jit(solution)/shard_map/psum | solution.py:47
  103.4 8.4 %gather_fusion = f32[512]{0:T(512)S(1)} fusion(f32[512,512]{0,1:T(8,128)} %all-reduce.4.cloned.1.call-done, s32[512]{0:T(512)S(1)} %bitcast.100), kind=kCustom, calls=%fused_computation | custom fusion | bytes 8192 | tf_op jit(solution)/shard_map/jit(diagonal)/cond/branch_0_fun/gather | solution.py:48
  113.7 11.7 %cholesky.130 = f32[128,128]{1,0:T(8,128)S(1)} custom-call(f32[128,128]{1,0:T(8,128)S(1)} %cholesky.194), custom_call_target="Cholesky" | custom-call | tf_op jit(solution)/shard_map/jit(cholesky)/cholesky | solution.py:31
  125.4 9.8 %custom-call.21 = f32[1,128,128]{1,2,0:T(8,128)S(1)} custom-call(f32[1,128,128]{2,1,0:T(8,128)S(1)} %get-tuple-element.67), custom_call_target="InvertDiagBlocksLowerTriangular" | custom-call | tf_op jit(solution)/shard_map/jit(cholesky)/cholesky | solution.py:31
  135.8 11.7 %cholesky.147 = f32[128,128]{1,0:T(8,128)S(1)} custom-call(f32[128,128]{1,0:T(8,128)S(1)} %convolution_subtract_fusion.5), custom_call_target="Cholesky" | custom-call | tf_op jit(solution)/shard_map/jit(cholesky)/cholesky | solution.py:31
  149.5 3.8 while.8
  153.3 20.2 %custom-call.23 = f32[2,128,128]{1,2,0:T(8,128)S(1)} custom-call(f32[2,128,128]{2,1,0:T(8,128)S(1)} %get-tuple-element.37), custom_call_target="InvertDiagBlocksLowerTriangular" | custom-call | tf_op jit(solution)/shard_map/triangular_solve/custom-call.4 | solution.py:21
  176.9 3.7 fusion.7
  180.6 2.1 fusion.4
  184.9 3.6 convolution_add_fusion.3
  188.6 23.5 %collective-permute-done = f32[2048,256]{0,1:T(8,128)S(1)} collective-permute-done((f32[2048,256]{0,1:T(8,128)S(1)}, f32[2048,256]{0,1:T(8,128)S(1)}, u32[]{:S(2)}, u32[]{:S(2)}) %collective-permute-start) | collective-permute-done | bytes 2097184 | tf_op jit(solution)/shard_map/ppermute | solution.py:12
  213.4 8.2 %fusion = f32[512,512]{0,1:T(8,128)} fusion(f32[2048,256]{0,1:T(8,128)S(1)} %collective-permute-done, f32[2048,256]{0,1:T(8,128)S(1)} %bitcast.102), kind=kOutput, calls=%fused_computation.6 | convolution fusion | flops 6443499520 | bytes 5242880 | tf_op jit(solution)/shard_map/dot_general | solution.py:16
  221.6 80.6 %all-reduce.6.cloned.1.call-done = f32[512,512]{0,1:T(8,128)} async-done(((f32[512,512]{0,1:T(8,128)}), f32[512,512]{0,1:T(8,128)}) %all-reduce.6.cloned.1.call-update) | async-done | bytes 1048592 | tf_op jit(solution)/shard_map/psum | solution.py:47
  302.2 8.4 %gather_fusion.1 = f32[512]{0:T(512)S(1)} fusion(f32[512,512]{0,1:T(8,128)} %all-reduce.6.cloned.1.call-done, s32[512]{0:T(512)S(1)} %bitcast.101), kind=kCustom, calls=%fused_computation.1 | custom fusion | bytes 8192 | tf_op jit(solution)/shard_map/jit(diagonal)/cond/branch_0_fun/gather | solution.py:48
  312.5 11.7 %cholesky.164 = f32[128,128]{1,0:T(8,128)S(1)} custom-call(f32[128,128]{1,0:T(8,128)S(1)} %cholesky.197), custom_call_target="Cholesky" | custom-call | tf_op jit(solution)/shard_map/jit(cholesky)/cholesky | solution.py:31
  325.0 9.8 %custom-call.24 = f32[1,128,128]{1,2,0:T(8,128)S(1)} custom-call(f32[1,128,128]{2,1,0:T(8,128)S(1)} %get-tuple-element.63), custom_call_target="InvertDiagBlocksLowerTriangular" | custom-call | tf_op jit(solution)/shard_map/jit(cholesky)/cholesky | solution.py:31
  335.3 11.7 %cholesky.181 = f32[128,128]{1,0:T(8,128)S(1)} custom-call(f32[128,128]{1,0:T(8,128)S(1)} %convolution_subtract_fusion.4), custom_call_target="Cholesky" | custom-call | tf_op jit(solution)/shard_map/jit(cholesky)/cholesky | solution.py:31
  349.0 4.1 while.9
  353.1 20.1 %custom-call.26 = f32[2,128,128]{1,2,0:T(8,128)S(1)} custom-call(f32[2,128,128]{2,1,0:T(8,128)S(1)} %get-tuple-element.39), custom_call_target="InvertDiagBlocksLowerTriangular" | custom-call | tf_op jit(solution)/shard_map/triangular_solve/custom-call.4 | solution.py:21
  383.0 2.1 convolution_add_fusion.1
  385.1 24.9 %collective-permute-done.1 = f32[2048,256]{0,1:T(8,128)S(1)} collective-permute-done((f32[2048,256]{0,1:T(8,128)S(1)}, f32[2048,256]{0,1:T(8,128)S(1)}, u32[]{:S(2)}, u32[]{:S(2)}) %collective-permute-start.1) | collective-permute-done | bytes 2097184 | tf_op jit(solution)/shard_map/ppermute | solution.py:12
  410.0 2.4 pad_maximum_fusion
  412.4 5.3 %copy.27 = f32[2048,512]{1,0:T(8,128)} copy(f32[2048,512]{0,1:T(8,128)} %pad_maximum_fusion) | data formatting | bytes 8388608 | tf_op jit(solution)/shard_map/concatenate | solution.py:67
  (77 shorter events, 31.8 us)
Async XLA Ops:
  6.5 96.8 %all-reduce.4.cloned.1.call-start = ((), (), s32[]{:S(2)}) async-start(), calls=%async_computation | async-start | bytes 2097152 | tf_op jit(solution)/shard_map/psum | solution.py:47
  17.7 284.5 %all-reduce.6.cloned.1.call-start = ((), (), s32[]{:S(2)}) async-start(), calls=%async_computation.1 | async-start | bytes 2097152 | tf_op jit(solution)/shard_map/psum | solution.py:47
  176.9 3.7 copy-start
  182.7 29.3 %collective-permute-start = (f32[2048,256]{0,1:T(8,128)S(1)}, f32[2048,256]{0,1:T(8,128)S(1)}, u32[]{:S(2)}, u32[]{:S(2)}) collective-permute-start(f32[2048,256]{0,1:T(8,128)S(1)} %fusion.4), channel_id=1, source_target_pairs={{0,8},{8,16},{16,24},{24,32},{32,40},{40,48},{48,56},{56,64},{64,7... | collective-permute-start | bytes 6291464 | tf_op jit(solution)/shard_map/ppermute | solution.py:12
  212.0 1.3 copy-start.1
  376.5 2.1 copy-start.2
  380.7 29.3 %collective-permute-start.1 = (f32[2048,256]{0,1:T(8,128)S(1)}, f32[2048,256]{0,1:T(8,128)S(1)}, u32[]{:S(2)}, u32[]{:S(2)}) collective-permute-start(f32[2048,256]{0,1:T(8,128)S(1)} %convolution_add_fusion), channel_id=1, source_target_pairs={{0,8},{8,16},{16,24},{24,32},{32,40},{40,48},{48,56},{56,64},{64,7... | collective-permute-start | bytes 6291464 | tf_op jit(solution)/shard_map/ppermute | solution.py:12
Sparse Core Ops, SparseCore 0:
  17.8 85.4 all-reduce.3
  221.7 80.4 all-reduce.5
where the time goes:
time: 429 us; the launch traced here: 425 us
  waiting for transfers between devices  214 us (50%)
  other arithmetic  114 us (27%)
  matrix products  47.5 us (11%)
  local copies, waits for them, and re-layouts  32 us (7%)
  between operations  16.5 us (4%)
    psum x2, waiting for transfers between devices, gram_terms(): summed = lax.psum(product(whole_pair.T, whole_pair), 'narrow')  166 us
    another operation x13, other arithmetic, turn_pair(): left_factor = jnp.linalg.cholesky(identity + left_square)  68.6 us
    ppermute x2, waiting for transfers between devices, from_behind(): return lax.ppermute(value, axis, pairs)  48.4 us
    dot_general x14, matrix products, product(): return jnp.dot(left, right, precision=lax.Precision.HIGHEST)  41 us
    another operation x5, other arithmetic, spd_solve(): lax.linalg.triangular_solve(factor_low, first_pass, left_side=True, lower...  40.3 us
    gather x2, local copies, waits for them, and re-layouts, gram_terms(): diagonal = jnp.diagonal(summed)  16.8 us
  transfers between devices with their start and end apart: 4, of which 4 were waited for; matrix products, arithmetic and copies ran while one was open for 2% of the time, Pallas kernels for 0%

commit v1 on v0

--- a/solution.py
+++ b/solution.py
@@ -4,6 +4,10 @@
 from jax.sharding import PartitionSpec as P
 
 STEPS = 2
+
+
+def recast_lane(target):
+    return jnp.sum(lax.all_gather(target, axis_name="narrow"), 0)
 
 
 def from_behind(value, axis, steps):
@@ -44,7 +48,7 @@
 def gram_terms(upper_block, pieces):
     block_width = upper_block.shape[1]
     whole_pair = jnp.concatenate((upper_block,) + pieces, axis=1)
-    summed = lax.psum(product(whole_pair.T, whole_pair), "narrow")
+    summed = recast_lane(product(whole_pair.T, whole_pair))
     diagonal = jnp.diagonal(summed)
     return (summed[:block_width, block_width:], diagonal[:block_width], diagonal[block_width:])
 

time: 429 us -> 614 us (1.43)
  waiting for transfers between devices: 214 us -> 393 us
  other arithmetic: 114 us -> 121 us
    all_gather x0 -> x2, waiting for transfers between devices: none -> 345 us  [recast_lane(): return jnp.sum(lax.all_gather(target, axis_name='narrow'), 0)]
    psum x2 -> x0, waiting for transfers between devices: 166 us -> none  [gram_terms(): summed = lax.psum(product(whole_pair.T, whole_pair), 'narrow')]
    reduce_sum x0 -> x2, other arithmetic: none -> 9.07 us  [recast_lane(): return jnp.sum(lax.all_gather(target, axis_name='narrow'), 0)]
    gather x2, local copies, waits for them, and re-layouts: 16.8 us -> 9.33 us  [gram_terms(): diagonal = jnp.diagonal(summed)]
where the time goes in v1:
time: 614 us; the launch traced here: 605 us
  waiting for transfers between devices  393 us (64%)
  other arithmetic  121 us (20%)
  matrix products  47.1 us (8%)
  local copies, waits for them, and re-layouts  26.5 us (4%)
  between operations  16.6 us (3%)
    all_gather x2, waiting for transfers between devices, recast_lane(): return jnp.sum(lax.all_gather(target, axis_name='narrow'), 0)  345 us
    another operation x13, other arithmetic, turn_pair(): left_factor = jnp.linalg.cholesky(identity + left_square)  68.6 us
    ppermute x2, waiting for transfers between devices, from_behind(): return lax.ppermute(value, axis, pairs)  48.5 us
    dot_general x14, matrix products, product(): return jnp.dot(left, right, precision=lax.Precision.HIGHEST)  40.6 us
    another operation x5, other arithmetic, spd_solve(): lax.linalg.triangular_solve(factor_low, first_pass, left_side=True, lower...  40.3 us
  transfers between devices with their start and end apart: 4, of which 4 were waited for; matrix products, arithmetic and copies ran while one was open for 2% of the time, Pallas kernels for 0%

profile of v1, /device:TPU:16, one launch (start us, length us, event | category | flops | bytes accessed | tf_op | source)
XLA Modules:
  0.0 605.2 jit_solution(1182759146424132403)
XLA Ops:
  6.5 11.1 %fusion.69 = f32[512,512]{1,0:T(8,128)} fusion(f32[2048,512]{1,0:T(8,128)} %param.6), kind=kOutput, calls=%fused_computation.131 | convolution fusion | flops 6442450944 | bytes 5242880 | tf_op jit(solution)/shard_map/dot_general | solution.py:20
  17.7 173.4 %all-gather.5.cloned.1.call-done = f32[4096,512]{1,0:T(8,128)} async-done(((f32[512,512]{1,0:T(8,128)}), f32[4096,512]{1,0:T(8,128)}) %all-gather.5.cloned.1.call-update) | async-done | bytes 8388624 | tf_op jit(solution)/shard_map/all_gather | solution.py:10
  191.2 4.5 reduce_sum.18
  195.7 4.8 gather_fusion
  201.6 11.7 %cholesky.130 = f32[128,128]{1,0:T(8,128)S(1)} custom-call(f32[128,128]{1,0:T(8,128)S(1)} %cholesky.194), custom_call_target="Cholesky" | custom-call | tf_op jit(solution)/shard_map/jit(cholesky)/cholesky | solution.py:35
  213.4 9.8 %custom-call.21 = f32[1,128,128]{1,2,0:T(8,128)S(1)} custom-call(f32[1,128,128]{2,1,0:T(8,128)S(1)} %get-tuple-element.67), custom_call_target="InvertDiagBlocksLowerTriangular" | custom-call | tf_op jit(solution)/shard_map/jit(cholesky)/cholesky | solution.py:35
  223.7 11.7 %cholesky.147 = f32[128,128]{1,0:T(8,128)S(1)} custom-call(f32[128,128]{1,0:T(8,128)S(1)} %convolution_subtract_fusion.5), custom_call_target="Cholesky" | custom-call | tf_op jit(solution)/shard_map/jit(cholesky)/cholesky | solution.py:35
  237.5 4.0 while.8
  241.5 20.2 %custom-call.23 = f32[2,128,128]{1,2,0:T(8,128)S(1)} custom-call(f32[2,128,128]{2,1,0:T(8,128)S(1)} %get-tuple-element.37), custom_call_target="InvertDiagBlocksLowerTriangular" | custom-call | tf_op jit(solution)/shard_map/triangular_solve/custom-call.4 | solution.py:25
  265.1 3.6 fusion.7
  272.9 3.6 convolution_add_fusion.3
  276.5 23.5 %collective-permute-done = f32[2048,256]{0,1:T(8,128)S(1)} collective-permute-done((f32[2048,256]{0,1:T(8,128)S(1)}, f32[2048,256]{0,1:T(8,128)S(1)}, u32[]{:S(2)}, u32[]{:S(2)}) %collective-permute-start) | collective-permute-done | bytes 2097184 | tf_op jit(solution)/shard_map/ppermute | solution.py:16
  301.3 8.2 %fusion = f32[512,512]{1,0:T(8,128)} fusion(f32[2048,256]{0,1:T(8,128)S(1)} %collective-permute-done, f32[2048,256]{0,1:T(8,128)S(1)} %bitcast.104), kind=kOutput, calls=%fused_computation.6 | convolution fusion | flops 6443499520 | bytes 5242880 | tf_op jit(solution)/shard_map/dot_general | solution.py:20
  309.6 171.5 %all-gather.7.cloned.1.call-done = f32[4096,512]{1,0:T(8,128)} async-done(((f32[512,512]{1,0:T(8,128)}), f32[4096,512]{1,0:T(8,128)}) %all-gather.7.cloned.1.call-update) | async-done | bytes 8388624 | tf_op jit(solution)/shard_map/all_gather | solution.py:10
  481.1 4.5 reduce_sum.19
  486.3 4.5 gather_fusion.1
  492.9 11.7 %cholesky.164 = f32[128,128]{1,0:T(8,128)S(1)} custom-call(f32[128,128]{1,0:T(8,128)S(1)} %cholesky.197), custom_call_target="Cholesky" | custom-call | tf_op jit(solution)/shard_map/jit(cholesky)/cholesky | solution.py:35
  504.7 9.8 %custom-call.24 = f32[1,128,128]{1,2,0:T(8,128)S(1)} custom-call(f32[1,128,128]{2,1,0:T(8,128)S(1)} %get-tuple-element.63), custom_call_target="InvertDiagBlocksLowerTriangular" | custom-call | tf_op jit(solution)/shard_map/jit(cholesky)/cholesky | solution.py:35
  514.9 11.7 %cholesky.181 = f32[128,128]{1,0:T(8,128)S(1)} custom-call(f32[128,128]{1,0:T(8,128)S(1)} %convolution_subtract_fusion.4), custom_call_target="Cholesky" | custom-call | tf_op jit(solution)/shard_map/jit(cholesky)/cholesky | solution.py:35
  529.4 4.1 while.9
  533.4 20.1 %custom-call.26 = f32[2,128,128]{1,2,0:T(8,128)S(1)} custom-call(f32[2,128,128]{2,1,0:T(8,128)S(1)} %get-tuple-element.39), custom_call_target="InvertDiagBlocksLowerTriangular" | custom-call | tf_op jit(solution)/shard_map/triangular_solve/custom-call.4 | solution.py:25
  565.4 25.0 %collective-permute-done.1 = f32[2048,256]{0,1:T(8,128)S(1)} collective-permute-done((f32[2048,256]{0,1:T(8,128)S(1)}, f32[2048,256]{0,1:T(8,128)S(1)}, u32[]{:S(2)}, u32[]{:S(2)}) %collective-permute-start.1) | collective-permute-done | bytes 2097184 | tf_op jit(solution)/shard_map/ppermute | solution.py:16
  590.4 2.4 pad_maximum_fusion
  592.8 5.3 copy.59
  (83 shorter events, 35.6 us)
Async XLA Ops:
  6.5 184.6 %all-gather.5.cloned.1.call-start = ((), (), s32[]{:S(2)}) async-start(), calls=%async_computation | async-start | bytes 9437184 | tf_op jit(solution)/shard_map/all_gather | solution.py:10
  17.6 463.5 %all-gather.7.cloned.1.call-start = ((), (), s32[]{:S(2)}) async-start(), calls=%async_computation.1 | async-start | bytes 9437184 | tf_op jit(solution)/shard_map/all_gather | solution.py:10
  265.1 3.7 copy-start
  270.7 29.3 %collective-permute-start = (f32[2048,256]{0,1:T(8,128)S(1)}, f32[2048,256]{0,1:T(8,128)S(1)}, u32[]{:S(2)}, u32[]{:S(2)}) collective-permute-start(f32[2048,256]{0,1:T(8,128)S(1)} %fusion.4), channel_id=1, source_target_pairs={{0,8},{8,16},{16,24},{24,32},{32,40},{40,48},{48,56},{56,64},{64,7... | collective-permute-start | bytes 6291464 | tf_op jit(solution)/shard_map/ppermute | solution.py:16
  300.0 1.3 copy-start.1
  557.0 2.1 copy-start.2
  561.0 29.3 %collective-permute-start.1 = (f32[2048,256]{0,1:T(8,128)S(1)}, f32[2048,256]{0,1:T(8,128)S(1)}, u32[]{:S(2)}, u32[]{:S(2)}) collective-permute-start(f32[2048,256]{0,1:T(8,128)S(1)} %convolution_add_fusion), channel_id=1, source_target_pairs={{0,8},{8,16},{16,24},{24,32},{32,40},{40,48},{48,56},{56,64},{64,7... | collective-permute-start | bytes 6291464 | tf_op jit(solution)/shard_map/ppermute | solution.py:16
Sparse Core Ops, SparseCore 0:
  17.8 173.3 all-gather.4
  309.7 171.3 all-gather.6
